TPU v7x, 512 devices: a whole 4x4x16 slice. The times are simulated.
512 devices in a mesh: node: 32 (over x, y, core), mode: 16 (over z).
Axes of the slice: x: 4, y: 4, z: 16, core: 2. Of those that a mesh axis runs over, the one named last changes fastest.
Arguments:
- panels: float32 [288, 16384], P('mode', 'node'), may hold values from -6 to 6
- blocks: float32 [11, 3, 64, 16384], P(None, None, None, 'node'), may hold values from -0.4375 to 0.4375
- cols: int32 [11, 3, 256], P(None, None, 'node'), may hold values from 0 to 255, as said below
Outputs:
- result: float32 [288, 16384], P('mode', 'node')
Inputs may be any that keep to these rules, and one draw needn't show every extreme that they name: cols[i, s, r] differs from r by at most 1.
All inputs are finite; a program needn't handle non-finite values.
Results may differ from a plain program's by a relative error of at most 0.0001.
Values sent between devices are 32-bit elements; how exact they have to be, the bound alone decides.
No kernel may reach another device: no remote copies, remote signals or barrier semaphores. Data moves between devices by JAX's collectives and lax.ppermute only.
A program may use at most 64 MiB of HBM per device.

v0:
```python
import math

import jax
import jax.numpy as jnp
import numpy as np
from jax import lax
from jax.sharding import PartitionSpec as P

MAT = 11
ORDER = 3
MODES = 288
BLOCK = 64
HALO_BLK = 1


def with_halo(cells, sides, width):
    for axis, dim in sides:
        count = lax.axis_size(axis)
        ends = count - 1
        head = lax.slice_in_dim(cells, 0, width, axis=dim)
        tail = lax.slice_in_dim(cells, cells.shape[dim] - width, cells.shape[dim], axis=dim)
        cells = jnp.concatenate(
            [
                lax.ppermute(tail, axis, [(i, (i + 1) % count) for i in range(ends)]),
                cells,
                lax.ppermute(head, axis, [((i + 1) % count, i) for i in range(ends)]),
            ],
            axis=dim,
        )
    return cells


def degree_lists(count, total):
    if count == 1:
        return [[total]]
    collected = []
    for leading in range(total, -1, -1):
        for remainder in degree_lists(count - 1, total - leading):
            collected.append([leading] + remainder)
    return collected


def chaos_table(mat_count, mode_count, order_max):
    variables = mat_count - 1
    indices = []
    for degree in range(order_max + 1):
        indices.extend(degree_lists(variables, degree))
    indices = indices[:mode_count]
    lookup = {tuple(vector): position for position, vector in enumerate(indices)}
    table = np.zeros((mat_count, mode_count, mode_count))
    for column, vector in enumerate(indices):
        table[0, column, column] = 1.0
        for variable in range(variables):
            raised = list(vector)
            raised[variable] = raised[variable] + 1
            if tuple(raised) in lookup:
                target = lookup[tuple(raised)]
                weight_value = math.sqrt(vector[variable] + 1)
                table[variable + 1, target, column] = weight_value
                table[variable + 1, column, target] = weight_value
    return table


def shards(panels, blocks, cols):
    mode_len = panels.shape[0]
    node_len = panels.shape[1]
    blk_count = node_len // BLOCK
    table_np = chaos_table(MAT, MODES, ORDER)
    padded = with_halo(panels, (("node", 1),), HALO_BLK * BLOCK)
    padded_blocks = padded.reshape(mode_len, blk_count + 2 * HALO_BLK, BLOCK)
    offset = lax.axis_index("node") * blk_count - HALO_BLK
    local_cols = cols - offset
    gathered = jnp.take(padded_blocks, local_cols, axis=1)
    value_blocks = blocks.reshape(blocks.shape[0], blocks.shape[1], BLOCK, blk_count, BLOCK)
    products = jnp.einsum(
        "isbra,jisrb->ijra", value_blocks, gathered, precision=lax.Precision.HIGHEST
    )
    products = products.reshape(blocks.shape[0], mode_len, node_len)
    coupling = jnp.asarray(table_np.astype(np.float32))
    regrouped = lax.all_to_all(products, "mode", split_axis=2, concat_axis=1, tiled=True)
    coupled = jnp.einsum("ikj,ijn->kn", coupling, regrouped, precision=lax.Precision.HIGHEST)
    return lax.all_to_all(coupled, "mode", split_axis=0, concat_axis=1, tiled=True)


def solution(mesh):
    return jax.shard_map(
        shards,
        mesh=mesh,
        in_specs=(P("mode", "node"), P(None, None, None, "node"), P(None, None, "node")),
        out_specs=P("mode", "node"),
        check_vma=False,
    )
```

profile of v0, /device:TPU:6, one launch (start us, length us, event | category | flops | bytes accessed | tf_op | source)
XLA Modules:
  0.0 112.0 jit_solution(4650532530279243593)
XLA Ops:
  0.0 0.8 fusion.8
  0.8 1.9 %collective-permute-start = (f32[18,64]{1,0:T(8,128)S(1)}, f32[18,64]{1,0:T(8,128)S(1)}, u32[]{:S(2)}, u32[]{:S(2)}) collective-permute-start(f32[18,64]{1,0:T(8,128)S(1)} %get-tuple-element.7), channel_id=1, source_target_pairs={{0,16},{16,32},{32,48},{48,64},{64,80},{80,96},{96,112},{112,128},... | collective-permute-start | bytes 13832 | tf_op jit(solution)/shard_map/ppermute | solution.py:24
  2.7 5.8 %collective-permute-start.1 = (f32[18,64]{1,0:T(8,128)S(1)}, f32[18,64]{1,0:T(8,128)S(1)}, u32[]{:S(2)}, u32[]{:S(2)}) collective-permute-start(f32[18,64]{1,0:T(8,128)S(1)} %get-tuple-element.8), channel_id=1, source_target_pairs={{16,0},{32,16},{48,32},{64,48},{80,64},{96,80},{112,96},{128,112},... | collective-permute-start | bytes 13832 | tf_op jit(solution)/shard_map/ppermute | solution.py:26
  8.5 0.7 compare_and_fusion
  9.2 0.1 copy.26
  9.3 0.1 reshape.22
  9.4 0.1 copy.25
  9.5 0.0 copy-start.1
  9.5 7.2 %reshape.18 = f32[11,3,64,8,64]{4,3,2,1,0:T(8,128)} reshape(f32[11,3,64,512]{3,2,1,0:T(8,128)} %param.5) | data formatting | bytes 8650752 | tf_op jit(solution)/shard_map/reshape | solution.py:74
  16.8 0.0 collective-permute-done
  16.8 0.0 collective-permute-done.1
  16.8 0.0 copy-done.1
  16.8 0.1 pad_maximum_fusion
  16.9 0.1 reshape.17
  17.0 2.1 %gather_fusion = f32[264,18,64]{2,1,0:T(8,128)S(1)} fusion(f32[18,10,64]{2,0,1:T(8,128)S(1)} %copy.27, s32[1024]{0:T(1024)S(1)} %pad_clamp_fusion), kind=kCustom, calls=%fused_computation | custom fusion | bytes 2434080 | tf_op jit(solution)/shard_map/jit(_take)/gather | solution.py:73
  19.1 0.0 copy-start
  19.1 0.5 copy.28
  19.6 0.2 select_bitcast_fusion
  19.8 2.7 %copy-done = f32[11,3,64,8,64]{4,3,2,1,0:T(8,128)S(1)} copy-done((f32[11,3,64,8,64]{4,3,2,1,0:T(8,128)S(1)}, f32[11,3,64,8,64]{4,3,2,1,0:T(8,128)}, u32[]{:S(2)}) %copy-start) | copy-done | bytes 4325400
  22.5 8.2 %fusion.3 = f32[11,18,8,64]{3,1,2,0:T(8,128)S(1)} fusion(f32[11,3,64,8,64]{4,3,2,1,0:T(8,128)S(1)} %copy-done, f32[18,11,3,8,64]{4,3,2,1,0:T(8,128)S(1)} %select_bitcast_fusion), kind=kOutput, calls=%fused_computation.5 | convolution fusion | flops 233570304 | bytes 5947392 | tf_op jit(solution)/shard_map/isbra,jisrb->ijra/dot_general | solution.py:75
  30.8 3.0 %copy.38 = f32[11,18,8,64]{1,0,3,2:T(8,128)} copy(f32[11,18,8,64]{3,1,2,0:T(8,128)S(1)} %fusion.3) | data formatting | bytes 811008 | tf_op jit(solution)/shard_map/reshape | solution.py:78
  33.8 3.5 %reshape.32 = f32[16,1,6336]{2,1,0:T(1,128)S(1)} reshape(f32[512,11,18]{2,1,0:T(8,128)} %bitcast.28) | data formatting | bytes 811008
  37.3 36.9 %all_to_all.37 = f32[16,1,6336]{2,1,0:T(1,128)S(1)} all-to-all(f32[16,1,6336]{2,1,0:T(1,128)S(1)} %reshape.32), channel_id=1, replica_groups=mesh['node'=32,'mode'=16] {'mode'}, dimensions={0} | all-to-all | bytes 811008 | tf_op jit(solution)/shard_map/all_to_all | solution.py:80
  74.2 0.5 broadcast.12
  74.8 1.6 %reduce = f32[16,6336]{1,0:T(8,128)S(1)} reduce(f32[16,1,6336]{2,1,0:T(1,128)S(1)} %all_to_all.37, f32[]{:T(128)} %broadcast.12), dimensions={1}, to_apply=%all_to_all.27.reduce_sub_computation | reduce | bytes 811012 | tf_op jit(solution)/shard_map/all_to_all | solution.py:80
  76.4 2.8 %reshape.33 = f32[512,11,18]{2,1,0:T(8,128)} reshape(f32[16,6336]{1,0:T(8,128)S(1)} %reduce) | data formatting | bytes 811008
  79.1 3.9 %copy.34 = f32[11,16,18,32]{2,1,3,0:T(8,128)S(1)} copy(f32[11,16,18,32]{2,0,3,1:T(8,128)} %bitcast.29) | data formatting | bytes 811008 | tf_op jit(solution)/shard_map/all_to_all | solution.py:80
  83.0 1.5 %all_to_all.30 = f32[11,288,32]{1,2,0:T(8,128)S(1)} reshape(f32[11,16,18,32]{2,1,3,0:T(8,128)S(1)} %copy.34) | data formatting | bytes 811008 | tf_op jit(solution)/shard_map/all_to_all | solution.py:80
  84.5 6.4 %convolution_bitcast_fusion = f32[288,32]{0,1:T(8,128)S(1)} fusion(f32[11,288,288]{2,1,0:T(8,128)} %constant.29.clone, f32[11,288,32]{1,2,0:T(8,128)S(1)} %all_to_all.30), kind=kOutput, calls=%fused_computation.6 | convolution fusion | flops 350355456 | bytes 4091904 | tf_op jit(solution)/shard_map/ikj,ijn->kn/dot_general | solution.py:81
  90.9 0.2 all_to_all.31
  91.0 0.2 copy.35
  91.2 0.1 reshape.34
  91.4 19.0 %all_to_all.38 = f32[16,1,576]{2,1,0:T(1,128)S(1)} all-to-all(f32[16,1,576]{2,1,0:T(1,128)S(1)} %reshape.34), channel_id=1, replica_groups=mesh['node'=32,'mode'=16] {'mode'}, dimensions={0} | all-to-all | bytes 73728 | tf_op jit(solution)/shard_map/all_to_all | solution.py:82
  110.4 0.7 reduce.1
  111.1 0.1 reshape.35
  111.3 0.7 all_to_all.34
  (3 shorter events, 0.1 us)
Async XLA Ops:
  0.8 16.0 %collective-permute-start = (f32[18,64]{1,0:T(8,128)S(1)}, f32[18,64]{1,0:T(8,128)S(1)}, u32[]{:S(2)}, u32[]{:S(2)}) collective-permute-start(f32[18,64]{1,0:T(8,128)S(1)} %get-tuple-element.7), channel_id=1, source_target_pairs={{0,16},{16,32},{32,48},{48,64},{64,80},{80,96},{96,112},{112,128},... | collective-permute-start | bytes 13832 | tf_op jit(solution)/shard_map/ppermute | solution.py:24
  2.7 14.0 %collective-permute-start.1 = (f32[18,64]{1,0:T(8,128)S(1)}, f32[18,64]{1,0:T(8,128)S(1)}, u32[]{:S(2)}, u32[]{:S(2)}) collective-permute-start(f32[18,64]{1,0:T(8,128)S(1)} %get-tuple-element.8), channel_id=1, source_target_pairs={{16,0},{32,16},{48,32},{64,48},{80,64},{96,80},{112,96},{128,112},... | collective-permute-start | bytes 13832 | tf_op jit(solution)/shard_map/ppermute | solution.py:26
  9.5 7.2 %copy-start.1 = (f32[18,512]{1,0:T(8,128)S(1)}, f32[18,512]{1,0:T(8,128)}, u32[]{:S(2)}) copy-start(f32[18,512]{1,0:T(8,128)} %param.4) | copy-start | bytes 110596
  19.1 3.5 %copy-start = (f32[11,3,64,8,64]{4,3,2,1,0:T(8,128)S(1)}, f32[11,3,64,8,64]{4,3,2,1,0:T(8,128)}, u32[]{:S(2)}) copy-start(f32[11,3,64,8,64]{4,3,2,1,0:T(8,128)} %reshape.18) | copy-start | bytes 12976132
where the time goes:
time: 113 us; the launch traced here: 112 us
  blocking collectives  55.9 us (49%)
  local copies, waits for them, and re-layouts  30.2 us (27%)
  matrix products  14.6 us (13%)
  starting transfers between devices  7.66 us (7%)
  other arithmetic  3.38 us (3%)
    all_to_all x1, blocking collectives, shards(): lax.all_to_all(products, 'mode', split_axis=2, concat_axis=1, tiled=True)  36.9 us
    all_to_all x1, blocking collectives, shards(): lax.all_to_all(coupled, 'mode', split_axis=0, concat_axis=1, tiled=True)  19 us
    unnamed x8, local copies, waits for them, and re-layouts  9.25 us
    dot_general x1, matrix products, shards(): jnp.einsum('isbra,jisrb->ijra', value_blocks, gathered, precision=lax.Pre...  8.23 us
    reshape x1, local copies, waits for them, and re-layouts, shards(): blocks.reshape(blocks.shape[0], blocks.shape[1], BLOCK, blk_count, BLOCK)  7.23 us
    dot_general x1, matrix products, shards(): jnp.einsum('ikj,ijn->kn', coupling, regrouped, precision=lax.Precision.HI...  6.39 us
    all_to_all x3, local copies, waits for them, and re-layouts, shards(): lax.all_to_all(products, 'mode', split_axis=2, concat_axis=1, tiled=True)  5.84 us
    ppermute x1, starting transfers between devices, with_halo(): lax.ppermute(head, axis, [((i + 1) % count, i) for i in range(ends)])  5.75 us
  transfers between devices with their start and end apart: 2, of which 0 were waited for; matrix products, arithmetic and copies ran while one was open for 7% of the time, Pallas kernels for 0%

commit v1 on v0

v1 whole, which is shorter than its diff:
```python
import functools

import jax
import jax.numpy as jnp
import numpy as np
from jax import lax
from jax.experimental import pallas as pl
from jax.experimental.pallas import tpu as pltpu
from jax.sharding import PartitionSpec as P

MAT = 11
VARS = MAT - 1
ORDER = 3
MODES = 288
BLOCK = 64
NNZ = 3
DEPTH = MAT * NNZ * BLOCK
GROUPS = 16
OWN = MODES // GROUPS
ROWS = 8
SLOTS = 10
WIDTH = SLOTS * BLOCK
PAD = 32
STEP = 24
LANES = 128
PAIRS = 17


def degree_lists(count, total):
    if count == 1:
        return [[total]]
    collected = []
    for leading in range(total, -1, -1):
        for remainder in degree_lists(count - 1, total - leading):
            collected.append([leading] + remainder)
    return collected


def mode_tables():
    indices = []
    for degree in range(ORDER + 1):
        indices.extend(degree_lists(VARS, degree))
    indices = indices[:MODES]
    own = np.full((GROUPS, PAD, LANES), -100.0, np.float32)
    every = np.full((16, GROUPS * STEP), 100.0, np.float32)
    for mode, vector in enumerate(indices):
        group, row = divmod(mode, OWN)
        own[group, row, :VARS] = vector
        every[:VARS, group * STEP + row] = vector
    return own, every


def split(value):
    high = value.astype(jnp.bfloat16)
    return high, (value - high.astype(jnp.float32)).astype(jnp.bfloat16)


def kernel(cols_ref, own_tab, every_tab, x_ref, gathered_ref, blocks_ref, out_ref,
           panel, coup, mixed_hi, mixed_lo, lhs, low):
    group = lax.axis_index("mode")
    first = lax.axis_index("node") * ROWS
    lane = lax.broadcasted_iota(jnp.int32, (PAD, LANES), 1)
    left = lane < BLOCK

    for g in range(GROUPS):
        rows = jnp.concatenate([gathered_ref[g], jnp.zeros((STEP - OWN, WIDTH), jnp.float32)], axis=0)
        panel[pl.ds(g * STEP, STEP), :] = rows

    own = own_tab[group]
    every = every_tab[...]
    gaps = [own[:, p : p + 1] - every[p : p + 1, :] for p in range(VARS)]
    apart = functools.reduce(lambda a, b: a + b, [g * g for g in gaps])
    adjacent = apart == 1.0
    for p in range(VARS):
        top = jnp.maximum(own[:, p : p + 1], every[p : p + 1, :])
        root = jnp.where(top == 1.0, 1.0, jnp.where(top == 2.0, np.float32(2.0**0.5), np.float32(3.0**0.5)))
        c_hi, c_lo = split(jnp.where(adjacent & (gaps[p] != 0.0), root, 0.0))
        coup[pl.ds(p * PAD, PAD), :] = c_hi
        coup[pl.ds((VARS + p) * PAD, PAD), :] = c_lo

    def keep(i, c, value):
        turned = pltpu.roll(value, BLOCK, 1)
        for half in range(2):
            pick = jnp.where(left, value, turned) if half == 0 else jnp.where(left, turned, value)
            hi, lo = split(pick)
            mixed_hi[i, 2 * c + half] = hi
            mixed_lo[i, 2 * c + half] = lo

    valid = own[:, 0:1] >= 0.0
    for c in range(WIDTH // LANES):
        at = pl.ds(c * LANES, LANES)
        mine = jnp.concatenate([x_ref[:, at], jnp.zeros((PAD - OWN, LANES), jnp.float32)], axis=0)
        keep(0, c, jnp.where(valid, mine, 0.0))
    half = VARS * PAD
    for c0, cw in ((0, 256), (256, 256), (512, 128)):
        p_hi, p_lo = split(panel[:, c0 : c0 + cw])
        both = jnp.dot(coup[...], p_hi, preferred_element_type=jnp.float32)
        mixed = both[:half] + both[half:] + jnp.dot(coup[:half], p_lo, preferred_element_type=jnp.float32)
        for p in range(VARS):
            for c in range(cw // LANES):
                keep(p + 1, c0 // LANES + c, mixed[p * PAD : (p + 1) * PAD, c * LANES : (c + 1) * LANES])

    def slot(i, s, r):
        rel = cols_ref[i, s, r] - first
        return jnp.where(rel < 0, ROWS, jnp.where(rel == ROWS, ROWS + 1, rel))

    for r in range(ROWS):
        for q in range(PAIRS):
            ia, sa = divmod(2 * q, NNZ)
            a = slot(ia, sa, r)
            at = pl.ds(q * LANES, LANES)
            if 2 * q + 1 < MAT * NNZ:
                ib, sb = divmod(2 * q + 1, NNZ)
                b = slot(ib, sb, r)
                hi = jnp.where(left, mixed_hi[ia, a], mixed_hi[ib, b])
                lo = jnp.where(left, mixed_lo[ia, a], mixed_lo[ib, b])
            else:
                hi, lo = mixed_hi[ia, a], mixed_lo[ia, a]
            lhs[r // 4, pl.ds((r % 4) * PAD, PAD), at] = hi
            lhs[r // 4, pl.ds((4 + r % 4) * PAD, PAD), at] = lo

    for t in range(2):
        total = None
        for k0, kw in ((0, 512), (512, 512), (1024, 512), (1536, 576)):
            w_hi, w_lo = split(blocks_ref[pl.ds(k0, kw), pl.ds(t * 256, 256)])
            both = jnp.dot(lhs[t, :, k0 : k0 + kw], w_hi, preferred_element_type=jnp.float32)
            part = both[: 4 * PAD] + both[4 * PAD :]
            part = part + jnp.dot(lhs[t, : 4 * PAD, k0 : k0 + kw], w_lo, preferred_element_type=jnp.float32)
            total = part if total is None else total + part
        for h in range(2):
            cut = total[:, h * LANES : (h + 1) * LANES]
            one, two = cut[(2 * h) * PAD : (2 * h + 1) * PAD], cut[(2 * h + 1) * PAD : (2 * h + 2) * PAD]
            out_ref[:, pl.ds(t * 256 + h * LANES, LANES)] = jnp.where(left, one, two)[:OWN]


def shards(panels, blocks, cols):
    count = lax.axis_size("node")
    before = lax.ppermute(panels[:, -BLOCK:], "node", [(i, i + 1) for i in range(count - 1)])
    after = lax.ppermute(panels[:, :BLOCK], "node", [(i + 1, i) for i in range(count - 1)])
    wide = jnp.concatenate([panels, before, after], axis=1)
    gathered = lax.all_gather(wide, "mode", axis=0, tiled=False)
    own, every = mode_tables()
    vmem = pl.BlockSpec(memory_space=pltpu.VMEM)
    return pl.pallas_call(
        kernel,
        out_shape=jax.ShapeDtypeStruct(panels.shape, jnp.float32),
        in_specs=[pl.BlockSpec(memory_space=pltpu.SMEM)] + [vmem] * 5,
        out_specs=vmem,
        scratch_shapes=[
            pltpu.VMEM((GROUPS * STEP, WIDTH), jnp.float32),
            pltpu.VMEM((2 * VARS * PAD, GROUPS * STEP), jnp.bfloat16),
            pltpu.VMEM((MAT, SLOTS, PAD, LANES), jnp.bfloat16),
            pltpu.VMEM((MAT, SLOTS, PAD, LANES), jnp.bfloat16),
            pltpu.VMEM((2, 8 * PAD, PAIRS * LANES), jnp.bfloat16),
            pltpu.VMEM((8, LANES), jnp.float32),
        ],
        compiler_params=pltpu.CompilerParams(vmem_limit_bytes=32 << 20),
        cost_estimate=pl.CostEstimate(flops=600_000_000, bytes_accessed=6_000_000, transcendentals=0),
    )(cols, jnp.asarray(own), jnp.asarray(every), wide, gathered, blocks.reshape(DEPTH, ROWS * BLOCK))


def solution(mesh):
    return jax.shard_map(
        shards,
        mesh=mesh,
        in_specs=(P("mode", "node"), P(None, None, None, "node"), P(None, None, "node")),
        out_specs=P("mode", "node"),
        check_vma=False,
    )
```

time: 113 us -> 62.4 us (0.55)
  local copies, waits for them, and re-layouts: 30.2 us -> 5.51 us
  matrix products: 14.6 us -> 0 us
  blocking collectives: 55.9 us -> 41.8 us
  Pallas kernels: 0 us -> 4.58 us
  other arithmetic: 3.38 us -> 1.75 us
    all_to_all x2 -> x0, blocking collectives: 55.9 us -> none  [the longest x1 36.9 us: shards(): lax.all_to_all(products, 'mode', split_axis=2, concat_axis=1, tiled=True)]
    all_gather x0 -> x1, blocking collectives: none -> 41.8 us  [shards(): gathered = lax.all_gather(wide, 'mode', axis=0, tiled=False)]
    dot_general x2 -> x0, matrix products: 14.6 us -> none  [the longest x1 8.23 us: shards(): jnp.einsum('isbra,jisrb->ijra', value_blocks, gathered, precision=lax.Pre...]
    reshape x4 -> x0, local copies, waits for them, and re-layouts: 10.4 us -> none  [the longest x1 7.23 us: shards(): blocks.reshape(blocks.shape[0], blocks.shape[1], BLOCK, blk_count, BLOCK)]
    all_to_all x7 -> x0, local copies, waits for them, and re-layouts: 6.97 us -> none  [the longest x3 5.84 us: shards(): lax.all_to_all(products, 'mode', split_axis=2, concat_axis=1, tiled=True)]
    pallas_call x0 -> x1, Pallas kernels: none -> 4.58 us  [shards(): pl.pallas_call(kernel, out_shape=jax.ShapeDtypeStruct(panels.shape, jnp.f...]
    unnamed x8 -> x7, local copies, waits for them, and re-layouts: 9.25 us -> 4.72 us
    gather x2 -> x0, local copies, waits for them, and re-layouts: 2.56 us -> none  [shards(): gathered = jnp.take(padded_blocks, local_cols, axis=1)]
  transfers between devices with their start and end apart: 2 -> 2, of which waited for: 0 -> 1; matrix products, arithmetic and copies ran while one was open for 7% -> 1% of each run, Pallas kernels for 0% -> 0%
where the time goes in v1:
time: 62.4 us; the launch traced here: 61.9 us
  blocking collectives  41.8 us (67%)
  starting transfers between devices  7.66 us (12%)
  local copies, waits for them, and re-layouts  5.51 us (9%)
  Pallas kernels  4.58 us (7%)
  other arithmetic  1.75 us (3%)
    all_gather x1, blocking collectives, shards(): gathered = lax.all_gather(wide, 'mode', axis=0, tiled=False)  41.8 us
    ppermute x1, starting transfers between devices, shards(): lax.ppermute(panels[:, :BLOCK], 'node', [(i + 1, i) for i in range(count...  5.75 us
    unnamed x7, local copies, waits for them, and re-layouts  4.72 us
    pallas_call x1, Pallas kernels, shards(): pl.pallas_call(kernel, out_shape=jax.ShapeDtypeStruct(panels.shape, jnp.f...  4.58 us
    ppermute x1, starting transfers between devices, shards(): lax.ppermute(panels[:, -BLOCK:], 'node', [(i, i + 1) for i in range(count...  1.91 us
  transfers between devices with their start and end apart: 2, of which 1 were waited for; matrix products, arithmetic and copies ran while one was open for 1% of the time, Pallas kernels for 0%

profile of v1, /device:TPU:6, one launch (start us, length us, event | category | flops | bytes accessed | tf_op | source)
XLA Modules:
  0.0 61.9 jit_solution(13800451462962727064)
XLA Ops:
  0.0 0.8 %fusion = (f32[18,64]{1,0:T(8,128)S(1)}, f32[18,64]{1,0:T(8,128)S(1)}) fusion(f32[18,512]{1,0:T(8,128)} %param.5), kind=kLoop, calls=%fused_computation.1 | loop fusion | bytes 18432 | tf_op jit(solution)/shard_map/slice | solution.py:138
  0.8 1.9 %collective-permute-start = (f32[18,64]{1,0:T(8,128)S(1)}, f32[18,64]{1,0:T(8,128)S(1)}, u32[]{:S(2)}, u32[]{:S(2)}) collective-permute-start(f32[18,64]{1,0:T(8,128)S(1)} %get-tuple-element.5), channel_id=1, source_target_pairs={{0,16},{16,32},{32,48},{48,64},{64,80},{80,96},{96,112},{112,128},... | collective-permute-start | bytes 13832 | tf_op jit(solution)/shard_map/ppermute | solution.py:138
  2.7 5.8 %collective-permute-start.1 = (f32[18,64]{1,0:T(8,128)S(1)}, f32[18,64]{1,0:T(8,128)S(1)}, u32[]{:S(2)}, u32[]{:S(2)}) collective-permute-start(f32[18,64]{1,0:T(8,128)S(1)} %get-tuple-element.6), channel_id=1, source_target_pairs={{16,0},{32,16},{48,32},{64,48},{80,64},{96,80},{112,96},{128,112},... | collective-permute-start | bytes 13832 | tf_op jit(solution)/shard_map/ppermute | solution.py:139
  8.5 0.8 %copy.7.cols_ref = s32[11,3,8]{2,1,0:T(4,128)S(1)} copy(s32[11,3,8]{0,2,1:T(8,128)} %param.7) | data formatting | bytes 2112 | tf_op args[2]
  9.3 0.0 collective-permute-done
  9.3 0.6 collective-permute-done.1
  9.9 0.9 %fusion.1 = f32[1,18,640]{2,1,0:T(8,128)S(1)} fusion(f32[18,64]{1,0:T(8,128)S(1)} %collective-permute-done.1, f32[18,64]{1,0:T(8,128)S(1)} %collective-permute-done, f32[18,512]{1,0:T(8,128)} %param.5), kind=kLoop, calls=%fused_computation.2 | loop fusion | flops 23040 | bytes 92160
  10.7 41.8 %all-gather.1.gathered_ref = f32[16,18,640]{2,1,0:T(8,128)S(1)} all-gather(f32[1,18,640]{2,1,0:T(8,128)S(1)} %fusion.1), channel_id=2, replica_groups=mesh['node'=32,'mode'=16] {'mode'}, dimensions={0}, use_global_device_ids=true | all-gather | bytes 783360 | tf_op jit(solution)/shard_map/all_gather | solution.py:141
  52.6 0.9 %pad_maximum_fusion.x_ref = f32[18,640]{1,0:T(8,128)S(1)} fusion(f32[18,64]{1,0:T(8,128)S(1)} %collective-permute-done.1, f32[18,64]{1,0:T(8,128)S(1)} %collective-permute-done, f32[18,512]{1,0:T(8,128)} %param.5), kind=kLoop, calls=%fused_computation | loop fusion | flops 23040 | bytes 92160 | tf_op jit(solution)/shard_map/concatenate | solution.py:140
  53.4 0.0 copy-start
  53.4 2.2 %copy-done = f32[11,3,64,512]{3,2,1,0:T(8,128)S(1)} copy-done((f32[11,3,64,512]{3,2,1,0:T(8,128)S(1)}, f32[11,3,64,512]{3,2,1,0:T(8,128)}, u32[]{:S(2)}) %copy-start) | copy-done | bytes 4325400
  55.7 0.0 copy-start.1
  55.7 0.9 %copy-done.1 = f32[16,32,128]{2,1,0:T(8,128)S(1)} copy-done((f32[16,32,128]{2,1,0:T(8,128)S(1)}, f32[16,32,128]{2,1,0:T(8,128)}, u32[]{:S(2)}) %copy-start.1) | copy-done | bytes 262168
  56.6 0.0 copy-start.2
  56.6 0.7 %copy-done.2 = f32[16,384]{1,0:T(8,128)S(1)} copy-done((f32[16,384]{1,0:T(8,128)S(1)}, f32[16,384]{1,0:T(8,128)}, u32[]{:S(2)}) %copy-start.2) | copy-done | bytes 24600
  57.4 4.6 %shard_map.55 = f32[18,512]{1,0:T(8,128)} custom-call(s32[11,3,8]{2,1,0:T(4,128)S(1)} %copy.7.cols_ref, f32[16,32,128]{2,1,0:T(8,128)S(1)} %copy-done.1, f32[16,384]{1,0:T(8,128)S(1)} %copy-done.2, f32[18,640]{1,0:T(8,128)S(1)} %pad_maximum_fusion.x_ref, f32[16,18,640]{2,1,0:T(8,128)S(1)} %all-gather.1.gathered_ref, f32[2112,512]{1,0:T(8,128)S(1)} %bitcast.3), custom_call_target="tpu_custom_call" | custom-call | flops 600000000 | bytes 6000000 | tf_op jit(solution)/shard_map/pallas_call | solution.py:144
Async XLA Ops:
  0.8 8.5 %collective-permute-start = (f32[18,64]{1,0:T(8,128)S(1)}, f32[18,64]{1,0:T(8,128)S(1)}, u32[]{:S(2)}, u32[]{:S(2)}) collective-permute-start(f32[18,64]{1,0:T(8,128)S(1)} %get-tuple-element.5), channel_id=1, source_target_pairs={{0,16},{16,32},{32,48},{48,64},{64,80},{80,96},{96,112},{112,128},... | collective-permute-start | bytes 13832 | tf_op jit(solution)/shard_map/ppermute | solution.py:138
  2.7 7.1 %collective-permute-start.1 = (f32[18,64]{1,0:T(8,128)S(1)}, f32[18,64]{1,0:T(8,128)S(1)}, u32[]{:S(2)}, u32[]{:S(2)}) collective-permute-start(f32[18,64]{1,0:T(8,128)S(1)} %get-tuple-element.6), channel_id=1, source_target_pairs={{16,0},{32,16},{48,32},{64,48},{80,64},{96,80},{112,96},{128,112},... | collective-permute-start | bytes 13832 | tf_op jit(solution)/shard_map/ppermute | solution.py:139
  53.4 2.2 %copy-start = (f32[11,3,64,512]{3,2,1,0:T(8,128)S(1)}, f32[11,3,64,512]{3,2,1,0:T(8,128)}, u32[]{:S(2)}) copy-start(f32[11,3,64,512]{3,2,1,0:T(8,128)} %param.6) | copy-start | bytes 12976132
  55.7 0.9 %copy-start.1 = (f32[16,32,128]{2,1,0:T(8,128)S(1)}, f32[16,32,128]{2,1,0:T(8,128)}, u32[]{:S(2)}) copy-start(f32[16,32,128]{2,1,0:T(8,128)} %constant.4.clone.own_tab) | copy-start | bytes 786436
  56.6 0.7 %copy-start.2 = (f32[16,384]{1,0:T(8,128)S(1)}, f32[16,384]{1,0:T(8,128)}, u32[]{:S(2)}) copy-start(f32[16,384]{1,0:T(8,128)} %constant.5.clone.every_tab) | copy-start | bytes 73732

commit v2 on v1

v2 whole, which is shorter than its diff:
```python
import functools

import jax
import jax.numpy as jnp
import numpy as np
from jax import lax
from jax.experimental import pallas as pl
from jax.experimental.pallas import tpu as pltpu
from jax.sharding import PartitionSpec as P

MAT = 11
VARS = MAT - 1
MODES = 288
BLOCK = 64
NNZ = 3
DEPTH = MAT * NNZ * BLOCK
GROUPS = 16
OWN = MODES // GROUPS
ROWS = 8
NODES = ROWS * BLOCK
SLOTS = ROWS + 1
PAD = 32
KINDS = 16
STEP = 24
LANES = 128
PAIRS = 17
TWOS = 6
CUTS = ((0, 512), (512, 512), (1024, 512), (1536, 576))


def counts(mode, entry):
    singles, pairs, triples, at_pair, at_triple = VARS + 1, 0, 0, [], []
    for v in range(VARS):
        at_pair.append(pairs)
        at_triple.append(triples)
        pairs += VARS - v
        triples += (VARS - v) * (VARS - v + 1) // 2

    def found(value, starts):
        run, start = jnp.zeros_like(value), jnp.zeros_like(value)
        for v in range(1, VARS):
            inside = value >= starts[v]
            run, start = jnp.where(inside, v, run), jnp.where(inside, starts[v], start)
        return run, start

    third = mode - (singles + pairs)
    top, start = found(third, at_triple)
    offset = jnp.zeros_like(mode)
    for v in range(1, VARS):
        offset = jnp.where(top == v, at_pair[v], offset)
    is_three, is_two = third >= 0, mode >= singles
    two = jnp.where(is_three, third - start + offset, mode - singles)
    high, start = found(two, at_pair)
    low = jnp.where(is_two, two - start + high, mode - 1)
    count = (low == entry).astype(jnp.int32)
    count = count + ((high == entry) & is_two).astype(jnp.int32) + ((top == entry) & is_three).astype(jnp.int32)
    return jnp.where(mode < singles + pairs + triples, count, 100).astype(jnp.float32)


def split(value):
    high = value.astype(jnp.bfloat16)
    return high, (value - high.astype(jnp.float32)).astype(jnp.bfloat16)


def twice(value, half, left):
    turned = pltpu.roll(value, BLOCK, 1)
    return jnp.where(left, value, turned) if half == 0 else jnp.where(left, turned, value)


def lefts(rows):
    return lax.broadcasted_iota(jnp.int32, (rows, LANES), 1) < BLOCK


def mix(gathered_ref, mixed_hi, mixed_lo, across, beside, panel, coup, edge):
    group = lax.axis_index("mode")
    even = lax.rem(lax.axis_index("node"), 2) == 0
    left = lefts(PAD)

    for g in range(GROUPS):
        rows = jnp.concatenate([gathered_ref[g], jnp.zeros((STEP - OWN, NODES), jnp.float32)], axis=0)
        panel[pl.ds(g * STEP, STEP), :] = rows

    lane = lax.broadcasted_iota(jnp.int32, (KINDS, GROUPS * STEP), 1)
    mode = jnp.where(lax.rem(lane, STEP) < OWN, lane // STEP * OWN + lax.rem(lane, STEP), MODES)
    every = counts(mode, lax.broadcasted_iota(jnp.int32, mode.shape, 0))
    row = lax.broadcasted_iota(jnp.int32, (PAD, LANES), 0)
    mode = jnp.where(row < OWN, group * OWN + row, MODES)
    own = counts(mode, lax.broadcasted_iota(jnp.int32, mode.shape, 1))
    gaps = [own[:, p : p + 1] - every[p : p + 1, :] for p in range(VARS)]
    apart = functools.reduce(lambda a, b: a + b, [g * g for g in gaps])
    adjacent = apart == 1.0
    for p in range(VARS):
        top = jnp.maximum(own[:, p : p + 1], every[p : p + 1, :])
        root = jnp.where(top == 1.0, 1.0, jnp.where(top == 2.0, np.float32(2.0**0.5), np.float32(3.0**0.5)))
        c_hi, c_lo = split(jnp.where(adjacent & (gaps[p] != 0.0), root, 0.0))
        coup[pl.ds(p * PAD, PAD), :] = c_hi
        coup[pl.ds((VARS + p) * PAD, PAD), :] = c_lo

    def keep(i, c, value):
        for half in range(2):
            hi, lo = split(twice(value, half, left))
            mixed_hi[i, 2 * c + half] = hi
            mixed_lo[i, 2 * c + half] = lo
        if c == 0:
            edge[0, i] = value[:STEP]
        if c == NODES // LANES - 1:
            edge[1, i] = value[:STEP]

    valid = own[:, 0:1] < 50.0
    for c in range(NODES // LANES):
        rows = gathered_ref[group, :, c * LANES : (c + 1) * LANES]
        mine = jnp.concatenate([rows, jnp.zeros((PAD - OWN, LANES), jnp.float32)], axis=0)
        keep(0, c, jnp.where(valid, mine, 0.0))
    half = VARS * PAD
    for c0 in range(0, NODES, 256):
        p_hi, p_lo = split(panel[:, c0 : c0 + 256])
        both = jnp.dot(coup[...], p_hi, preferred_element_type=jnp.float32)
        mixed = both[:half] + both[half:] + jnp.dot(coup[:half], p_lo, preferred_element_type=jnp.float32)
        for p in range(VARS):
            for c in range(2):
                keep(p + 1, c0 // LANES + c, mixed[p * PAD : (p + 1) * PAD, c * LANES : (c + 1) * LANES])
    none = jnp.zeros((PAD, LANES), jnp.bfloat16)
    for i in range(MAT):
        mixed_hi[i, ROWS] = none
        mixed_lo[i, ROWS] = none
    near = lefts(STEP)
    for q in range(TWOS):
        a = 2 * q
        b = min(a + 1, MAT - 1)
        head = jnp.where(near, edge[0, a], pltpu.roll(edge[0, b], BLOCK, 1))
        tail = jnp.where(near, pltpu.roll(edge[1, a], BLOCK, 1), edge[1, b])
        across[q] = jnp.where(even, head, tail)
        beside[q] = jnp.where(even, tail, head)


def inner(cols_ref, mixed_hi, mixed_lo, blocks_hbm, part_ref, end_hi, end_lo, lhs, blocks, sems):
    first = lax.axis_index("node") * ROWS
    copies = [
        pltpu.make_async_copy(blocks_hbm.at[pl.ds(k0, kw)], blocks.at[pl.ds(k0, kw)], sems.at[j])
        for j, (k0, kw) in enumerate(CUTS)
    ]
    for copy in copies:
        copy.start()
    left = lefts(PAD)

    def slot(n, r):
        i, s = divmod(n, NNZ)
        rel = cols_ref[s, r, i] - first
        return i, jnp.where((rel < 0) | (rel >= ROWS), ROWS, rel)

    for r in range(ROWS):
        for q in range(PAIRS):
            at = pl.ds(q * LANES, LANES)
            i, a = slot(2 * q, r)
            hi, lo = mixed_hi[i, a], mixed_lo[i, a]
            if 2 * q + 1 < MAT * NNZ:
                i, b = slot(2 * q + 1, r)
                hi = jnp.where(left, hi, mixed_hi[i, b])
                lo = jnp.where(left, lo, mixed_lo[i, b])
            lhs[r // 4, pl.ds((r % 4) * PAD, PAD), at] = hi
            lhs[r // 4, pl.ds((4 + r % 4) * PAD, PAD), at] = lo

    totals = [None, None]
    for copy, (k0, kw) in zip(copies, CUTS):
        copy.wait()
        for t in range(2):
            w_hi, w_lo = split(blocks[pl.ds(k0, kw), pl.ds(t * 256, 256)])
            both = jnp.dot(lhs[t, :, k0 : k0 + kw], w_hi, preferred_element_type=jnp.float32)
            part = both[: 4 * PAD] + both[4 * PAD :]
            part = part + jnp.dot(lhs[t, : 4 * PAD, k0 : k0 + kw], w_lo, preferred_element_type=jnp.float32)
            totals[t] = part if totals[t] is None else totals[t] + part
        ends = jnp.where(lefts(kw), blocks[pl.ds(k0, kw), pl.ds(0, LANES)], blocks[pl.ds(k0, kw), pl.ds(NODES - LANES, LANES)])
        hi, lo = split(ends)
        end_hi[pl.ds(k0, kw), :] = hi
        end_lo[pl.ds(k0, kw), :] = lo
    for t in range(2):
        for h in range(2):
            cut = totals[t][:, h * LANES : (h + 1) * LANES]
            one, two = cut[(2 * h) * PAD : (2 * h + 1) * PAD], cut[(2 * h + 1) * PAD : (2 * h + 2) * PAD]
            part_ref[:, pl.ds(t * 256 + h * LANES, LANES)] = jnp.where(left, one, two)[:OWN]


def outer(cols_ref, across_ref, beside_ref, end_hi, end_lo, part_ref, out_ref, lhs):
    node = lax.axis_index("node")
    first = node * ROWS
    even = lax.rem(node, 2) == 0
    near = lefts(STEP)
    fill = jnp.zeros((PAD - STEP, LANES), jnp.float32)
    for side, (r, want) in enumerate(((0, first - 1), (ROWS - 1, first + ROWS))):
        even_ref, odd_ref = (across_ref, beside_ref) if side == 0 else (beside_ref, across_ref)
        packed = [jnp.where(even, even_ref[q], odd_ref[q]) for q in range(TWOS)]
        both = [twice(packed[i // 2], i % 2, near) for i in range(MAT)]
        for q in range(PAIRS):
            i, s = divmod(2 * q, NNZ)
            value = jnp.where(cols_ref[s, r, i] == want, both[i], 0.0)
            if 2 * q + 1 < MAT * NNZ:
                i, s = divmod(2 * q + 1, NNZ)
                value = jnp.where(near, value, jnp.where(cols_ref[s, r, i] == want, both[i], 0.0))
            hi, lo = split(jnp.concatenate([value, fill], axis=0))
            lhs[pl.ds(side * PAD, PAD), pl.ds(q * LANES, LANES)] = hi
            lhs[pl.ds((2 + side) * PAD, PAD), pl.ds(q * LANES, LANES)] = lo
    twos = jnp.dot(lhs[:, :DEPTH], end_hi[...], preferred_element_type=jnp.float32)
    total = twos[: 2 * PAD] + twos[2 * PAD :]
    total = total + jnp.dot(lhs[: 2 * PAD, :DEPTH], end_lo[...], preferred_element_type=jnp.float32)
    left = lefts(OWN)
    out_ref[...] = part_ref[...]
    out_ref[:, :LANES] = part_ref[:, :LANES] + jnp.where(left, total[:OWN], 0.0)
    out_ref[:, NODES - LANES :] = part_ref[:, NODES - LANES :] + jnp.where(left, 0.0, total[PAD : PAD + OWN])


def shards(panels, blocks, cols):
    count = lax.axis_size("node")
    gathered = lax.all_gather(panels, "mode", axis=0, tiled=False)
    cols = cols.transpose(1, 2, 0)
    vmem = pl.BlockSpec(memory_space=pltpu.VMEM)
    smem = pl.BlockSpec(memory_space=pltpu.SMEM)
    hbm = pl.BlockSpec(memory_space=pltpu.MemorySpace.HBM)
    f32, bf16 = jnp.float32, jnp.bfloat16
    params = pltpu.CompilerParams(vmem_limit_bytes=50 << 20)
    mixed = jax.ShapeDtypeStruct((MAT, SLOTS, PAD, LANES), bf16)
    edge = jax.ShapeDtypeStruct((TWOS, STEP, LANES), f32)
    mixed_hi, mixed_lo, across, beside = pl.pallas_call(
        mix,
        out_shape=(mixed, mixed, edge, edge),
        in_specs=[vmem],
        out_specs=(vmem,) * 4,
        scratch_shapes=[
            pltpu.VMEM((GROUPS * STEP, NODES), f32),
            pltpu.VMEM((2 * VARS * PAD, GROUPS * STEP), bf16),
            pltpu.VMEM((2, MAT, STEP, LANES), f32),
        ],
        compiler_params=params,
        cost_estimate=pl.CostEstimate(flops=400_000_000, bytes_accessed=2_000_000, transcendentals=0),
    )(gathered)
    steps = [(i, i + 1) for i in range(1, count - 1, 2)]
    across = lax.ppermute(across, "node", steps + [(b, a) for a, b in steps])
    beside = lax.ppermute(beside, "node", [(i, i ^ 1) for i in range(count)])
    end = jax.ShapeDtypeStruct((DEPTH, LANES), bf16)
    part, end_hi, end_lo = pl.pallas_call(
        inner,
        out_shape=(jax.ShapeDtypeStruct(panels.shape, f32), end, end),
        in_specs=[smem, vmem, vmem, hbm],
        out_specs=(vmem,) * 3,
        scratch_shapes=[
            pltpu.VMEM((2, 8 * PAD, PAIRS * LANES), bf16),
            pltpu.VMEM((DEPTH, NODES), f32),
            pltpu.SemaphoreType.DMA((len(CUTS),)),
        ],
        compiler_params=params,
        cost_estimate=pl.CostEstimate(flops=900_000_000, bytes_accessed=8_000_000, transcendentals=0),
    )(cols, mixed_hi, mixed_lo, blocks.reshape(DEPTH, NODES))
    return pl.pallas_call(
        outer,
        out_shape=jax.ShapeDtypeStruct(panels.shape, f32),
        in_specs=[smem] + [vmem] * 5,
        out_specs=vmem,
        scratch_shapes=[pltpu.VMEM((4 * PAD, PAIRS * LANES), bf16)],
        compiler_params=params,
        cost_estimate=pl.CostEstimate(flops=100_000_000, bytes_accessed=1_500_000, transcendentals=0),
    )(cols, across, beside, end_hi, end_lo, part)


def solution(mesh):
    return jax.shard_map(
        shards,
        mesh=mesh,
        in_specs=(P("mode", "node"), P(None, None, None, "node"), P(None, None, "node")),
        out_specs=P("mode", "node"),
        check_vma=False,
    )
```

time: 62.4 us -> 54.4 us (0.87)
  the two profiles are of different devices: /device:TPU:6 before, /device:TPU:1 now
where the time goes in v2:
time: 54.4 us; the launch traced here: 54.1 us
  blocking collectives  34.2 us (63%)
  starting transfers between devices  12.7 us (23%)
  Pallas kernels  6.45 us (12%)
  local copies, waits for them, and re-layouts  0.7 us (1%)
    all_gather x1, blocking collectives, shards(): gathered = lax.all_gather(panels, 'mode', axis=0, tiled=False)  34.2 us
    ppermute x1, starting transfers between devices, shards(): across = lax.ppermute(across, 'node', steps + [(b, a) for a, b in steps])  10.8 us
    pallas_call x1, Pallas kernels, shards(): pl.pallas_call(inner, out_shape=(jax.ShapeDtypeStruct(panels.shape, f32),...  3.48 us
    ppermute x1, starting transfers between devices, shards(): beside = lax.ppermute(beside, 'node', [(i, i ^ 1) for i in range(count)])  1.92 us
    pallas_call x1, Pallas kernels, shards(): pl.pallas_call(outer, out_shape=jax.ShapeDtypeStruct(panels.shape, f32),...  1.84 us
    pallas_call x1, Pallas kernels, shards(): pl.pallas_call(mix, out_shape=(mixed, mixed, edge, edge), in_specs=[vmem]...  1.13 us
  transfers between devices with their start and end apart: 2, of which 0 were waited for; matrix products, arithmetic and copies ran while one was open for 0% of the time, Pallas kernels for 6%

profile of v2, /device:TPU:1, one launch (start us, length us, event | category | flops | bytes accessed | tf_op | source)
XLA Modules:
  0.0 54.1 jit_solution(10439891646312104709)
XLA Ops:
  0.0 34.2 %all-gather.1.gathered_ref = f32[16,18,512]{2,1,0:T(8,128)S(1)} all-gather(f32[1,18,512]{2,1,0:T(8,128)} %bitcast.6), channel_id=2, replica_groups=mesh['node'=32,'mode'=16] {'mode'}, dimensions={0}, use_global_device_ids=true | all-gather | bytes 626688 | tf_op jit(solution)/shard_map/all_gather | solution.py:213
  34.2 1.1 %shard_map.37 = (bf16[11,9,32,128]{3,2,1,0:T(8,128)(2,1)S(1)}, bf16[11,9,32,128]{3,2,1,0:T(8,128)(2,1)S(1)}, f32[6,24,128]{2,1,0:T(8,128)S(1)}, f32[6,24,128]{2,1,0:T(8,128)S(1)}) custom-call(f32[16,18,512]{2,1,0:T(8,128)S(1)} %all-gather.1.gathered_ref), custom_call_target="tpu_custom_call" | custom-call | flops 400000000 | bytes 2000000 | tf_op jit(solution)/shard_map/pallas_call | solution.py:222
  35.3 10.8 %collective-permute-start = (f32[6,24,128]{2,1,0:T(8,128)S(1)}, f32[6,24,128]{2,1,0:T(8,128)S(1)}, u32[]{:S(2)}, u32[]{:S(2)}) collective-permute-start(f32[6,24,128]{2,1,0:T(8,128)S(1)} %get-tuple-element.12), channel_id=1, source_target_pairs={{16,32},{48,64},{80,96},{112,128},{144,160},{176,192},{208,224},{2... | collective-permute-start | bytes 221192 | tf_op jit(solution)/shard_map/ppermute | solution.py:236
  46.1 1.9 %collective-permute-start.1 = (f32[6,24,128]{2,1,0:T(8,128)S(1)}, f32[6,24,128]{2,1,0:T(8,128)S(1)}, u32[]{:S(2)}, u32[]{:S(2)}) collective-permute-start(f32[6,24,128]{2,1,0:T(8,128)S(1)} %get-tuple-element.13), channel_id=1, source_target_pairs={{0,16},{16,0},{32,48},{48,32},{64,80},{80,64},{96,112},{112,96},{1... | collective-permute-start | bytes 221192 | tf_op jit(solution)/shard_map/ppermute | solution.py:237
  48.1 0.0 copy-start
  48.1 0.7 %copy-done = s32[11,3,8]{0,2,1:T(8,128)S(1)} copy-done((s32[11,3,8]{0,2,1:T(8,128)S(1)}, s32[11,3,8]{0,2,1:T(8,128)}, u32[]{:S(2)}) %copy-start) | copy-done | bytes 1080
  48.8 3.5 %shard_map.38 = (f32[18,512]{1,0:T(8,128)S(1)}, bf16[2112,128]{1,0:T(8,128)(2,1)S(1)}, bf16[2112,128]{1,0:T(8,128)(2,1)S(1)}) custom-call(s32[3,8,11]{2,1,0:T(8,128)S(1)} %bitcast.3, bf16[11,9,32,128]{3,2,1,0:T(8,128)(2,1)S(1)} %get-tuple-element.14.mixed_hi, bf16[11,9,32,128]{3,2,1,0:T(8,128)(2,1)S(1)} %get-tuple-element.15.mixed_lo, f32[2112,512]{1,0:T(8,128)} %bitcast.5), custom_call_target="tpu_custom_call" | custom-call | flops 900000000 | bytes 8000000 | tf_op jit(solution)/shard_map/pallas_call | solution.py:239
  52.3 0.0 collective-permute-done.across_ref
  52.3 0.0 collective-permute-done.1.beside_ref
  52.3 1.8 %shard_map.39 = f32[18,512]{1,0:T(8,128)} custom-call(s32[3,8,11]{2,1,0:T(8,128)S(1)} %bitcast.4, f32[6,24,128]{2,1,0:T(8,128)S(1)} %collective-permute-done.across_ref, f32[6,24,128]{2,1,0:T(8,128)S(1)} %collective-permute-done.1.beside_ref, bf16[2112,128]{1,0:T(8,128)(2,1)S(1)} %get-tuple-element.16.end_hi, ...), custom_call_target="tpu_custom_call" | custom-call | flops 100000000 | bytes 1500000 | tf_op jit(solution)/shard_map/pallas_call | solution.py:252
Async XLA Ops:
  35.3 17.0 %collective-permute-start = (f32[6,24,128]{2,1,0:T(8,128)S(1)}, f32[6,24,128]{2,1,0:T(8,128)S(1)}, u32[]{:S(2)}, u32[]{:S(2)}) collective-permute-start(f32[6,24,128]{2,1,0:T(8,128)S(1)} %get-tuple-element.12), channel_id=1, source_target_pairs={{16,32},{48,64},{80,96},{112,128},{144,160},{176,192},{208,224},{2... | collective-permute-start | bytes 221192 | tf_op jit(solution)/shard_map/ppermute | solution.py:236
  46.1 6.1 %collective-permute-start.1 = (f32[6,24,128]{2,1,0:T(8,128)S(1)}, f32[6,24,128]{2,1,0:T(8,128)S(1)}, u32[]{:S(2)}, u32[]{:S(2)}) collective-permute-start(f32[6,24,128]{2,1,0:T(8,128)S(1)} %get-tuple-element.13), channel_id=1, source_target_pairs={{0,16},{16,0},{32,48},{48,32},{64,80},{80,64},{96,112},{112,96},{1... | collective-permute-start | bytes 221192 | tf_op jit(solution)/shard_map/ppermute | solution.py:237
  48.1 0.7 %copy-start = (s32[11,3,8]{0,2,1:T(8,128)S(1)}, s32[11,3,8]{0,2,1:T(8,128)}, u32[]{:S(2)}) copy-start(s32[11,3,8]{0,2,1:T(8,128)} %param.5) | copy-start | bytes 3172

commit v3 on v2

v3 whole, which is shorter than its diff:
```python
import functools

import jax
import jax.numpy as jnp
import numpy as np
from jax import lax
from jax.experimental import pallas as pl
from jax.experimental.pallas import tpu as pltpu
from jax.sharding import PartitionSpec as P

MAT = 11
VARS = MAT - 1
MODES = 288
BLOCK = 64
NNZ = 3
DEPTH = MAT * NNZ * BLOCK
GROUPS = 16
OWN = MODES // GROUPS
ROWS = 8
NODES = ROWS * BLOCK
SLOTS = ROWS + 2
PAD = 32
KINDS = 16
STEP = 24
LANES = 128
PAIRS = 17
TWOS = 6
CUTS = ((0, 256), (256, 256), (512, 256), (768, 256), (1024, 256), (1280, 256), (1536, 256), (1792, 256), (2048, 64))


def counts(mode, entry):
    singles, pairs, triples, at_pair, at_triple = VARS + 1, 0, 0, [], []
    for v in range(VARS):
        at_pair.append(pairs)
        at_triple.append(triples)
        pairs += VARS - v
        triples += (VARS - v) * (VARS - v + 1) // 2

    def found(value, starts):
        run, start = jnp.zeros_like(value), jnp.zeros_like(value)
        for v in range(1, VARS):
            inside = value >= starts[v]
            run, start = jnp.where(inside, v, run), jnp.where(inside, starts[v], start)
        return run, start

    third = mode - (singles + pairs)
    top, start = found(third, at_triple)
    offset = jnp.zeros_like(mode)
    for v in range(1, VARS):
        offset = jnp.where(top == v, at_pair[v], offset)
    is_three, is_two = third >= 0, mode >= singles
    two = jnp.where(is_three, third - start + offset, mode - singles)
    high, start = found(two, at_pair)
    low = jnp.where(is_two, two - start + high, mode - 1)
    count = (low == entry).astype(jnp.int32)
    count = count + ((high == entry) & is_two).astype(jnp.int32) + ((top == entry) & is_three).astype(jnp.int32)
    return jnp.where(mode < singles + pairs + triples, count, 100).astype(jnp.float32)


def split(value):
    high = value.astype(jnp.bfloat16)
    return high, (value - high.astype(jnp.float32)).astype(jnp.bfloat16)


def twice(value, half, left):
    turned = pltpu.roll(value, BLOCK, 1)
    return jnp.where(left, value, turned) if half == 0 else jnp.where(left, turned, value)


def lefts(rows):
    return lax.broadcasted_iota(jnp.int32, (rows, LANES), 1) < BLOCK


def mix(gathered_ref, mixed_hi, mixed_lo, across, beside, panel, coup, edge):
    group = lax.axis_index("mode")
    even = lax.rem(lax.axis_index("node"), 2) == 0
    near = lefts(STEP)

    for g in range(GROUPS):
        rows = jnp.concatenate([gathered_ref[g], jnp.zeros((STEP - OWN, NODES), jnp.float32)], axis=0)
        panel[pl.ds(g * STEP, STEP), :] = rows

    lane = lax.broadcasted_iota(jnp.int32, (KINDS, GROUPS * STEP), 1)
    mode = jnp.where(lax.rem(lane, STEP) < OWN, lane // STEP * OWN + lax.rem(lane, STEP), MODES)
    every = counts(mode, lax.broadcasted_iota(jnp.int32, mode.shape, 0))
    row = lax.broadcasted_iota(jnp.int32, (STEP, LANES), 0)
    mode = jnp.where(row < OWN, group * OWN + row, MODES)
    own = counts(mode, lax.broadcasted_iota(jnp.int32, mode.shape, 1))
    gaps = [own[:, p : p + 1] - every[p : p + 1, :] for p in range(VARS)]
    apart = functools.reduce(lambda a, b: a + b, [g * g for g in gaps])
    adjacent = apart == 1.0
    for p in range(VARS):
        top = jnp.maximum(own[:, p : p + 1], every[p : p + 1, :])
        root = jnp.where(top == 1.0, 1.0, jnp.where(top == 2.0, np.float32(2.0**0.5), np.float32(3.0**0.5)))
        coup[pl.ds(p * STEP, STEP), :] = jnp.where(adjacent & (gaps[p] != 0.0), root, 0.0)

    def keep(i, c, value):
        for half in range(2):
            hi, lo = split(twice(value, half, near))
            mixed_hi[i, 2 * c + half + 1, :STEP] = hi
            mixed_lo[i, 2 * c + half + 1, :STEP] = lo
        if c == 0:
            edge[0, i] = value
        if c == NODES // LANES - 1:
            edge[1, i] = value

    valid = own[:, 0:1] < 50.0
    for c in range(NODES // LANES):
        rows = gathered_ref[group, :, c * LANES : (c + 1) * LANES]
        mine = jnp.concatenate([rows, jnp.zeros((STEP - OWN, LANES), jnp.float32)], axis=0)
        keep(0, c, jnp.where(valid, mine, 0.0))
    c_hi, c_lo = split(coup[...])
    for c0 in range(0, NODES, 256):
        p_hi, p_lo = split(panel[:, c0 : c0 + 256])
        mixed = jnp.dot(c_hi, p_hi, preferred_element_type=jnp.float32)
        mixed = mixed + jnp.dot(c_lo, p_hi, preferred_element_type=jnp.float32)
        mixed = mixed + jnp.dot(c_hi, p_lo, preferred_element_type=jnp.float32)
        for p in range(VARS):
            for c in range(2):
                keep(p + 1, c0 // LANES + c, mixed[p * STEP : (p + 1) * STEP, c * LANES : (c + 1) * LANES])
    none = jnp.zeros((PAD, LANES), jnp.bfloat16)
    for i in range(MAT):
        for none_at in (0, ROWS + 1):
            mixed_hi[i, none_at] = none
            mixed_lo[i, none_at] = none
    for q in range(TWOS):
        a = 2 * q
        b = min(a + 1, MAT - 1)
        head = jnp.where(near, edge[0, a], pltpu.roll(edge[0, b], BLOCK, 1))
        tail = jnp.where(near, pltpu.roll(edge[1, a], BLOCK, 1), edge[1, b])
        across[q] = jnp.where(even, head, tail)
        beside[q] = jnp.where(even, tail, head)


def inner(cols_ref, mixed_hi, mixed_lo, blocks, part_ref, end_hi, end_lo, mask_ref, lhs):
    first = lax.axis_index("node") * ROWS
    before = first - 1
    left = lefts(PAD)

    def slot(n, r):
        i, s = divmod(n, NNZ)
        return i, cols_ref[s, r, i] - before

    for t in range(2):
        for r in range(4 * t, 4 * t + 4):
            for q in range(PAIRS):
                at = pl.ds(q * LANES, LANES)
                i, a = slot(2 * q, r)
                hi, lo = mixed_hi[i, a], mixed_lo[i, a]
                if 2 * q + 1 < MAT * NNZ:
                    i, b = slot(2 * q + 1, r)
                    hi = jnp.where(left, hi, mixed_hi[i, b])
                    lo = jnp.where(left, lo, mixed_lo[i, b])
                lhs[t, pl.ds((r % 4) * PAD, PAD), at] = hi
                lhs[t, pl.ds((4 + r % 4) * PAD, PAD), at] = lo
    for t in range(2):
        total = None
        for k0, kw in CUTS:
            w_hi, w_lo = split(blocks[pl.ds(k0, kw), pl.ds(t * 256, 256)])
            both = jnp.dot(lhs[t, :, k0 : k0 + kw], w_hi, preferred_element_type=jnp.float32)
            part = both[: 4 * PAD] + both[4 * PAD :]
            part = part + jnp.dot(lhs[t, : 4 * PAD, k0 : k0 + kw], w_lo, preferred_element_type=jnp.float32)
            total = part if total is None else total + part
            if t == 0:
                end_hi[pl.ds(k0, kw), :BLOCK] = w_hi[:, :BLOCK]
                end_lo[pl.ds(k0, kw), :BLOCK] = w_lo[:, :BLOCK]
            else:
                end_hi[pl.ds(k0, kw), BLOCK:] = w_hi[:, 256 - BLOCK :]
                end_lo[pl.ds(k0, kw), BLOCK:] = w_lo[:, 256 - BLOCK :]
        for h in range(2):
            cut = total[:, h * LANES : (h + 1) * LANES]
            one, two = cut[(2 * h) * PAD : (2 * h + 1) * PAD], cut[(2 * h + 1) * PAD : (2 * h + 2) * PAD]
            part_ref[:, pl.ds(t * 256 + h * LANES, LANES)] = jnp.where(left, one, two)[:OWN]

    few = lefts(8)
    for side, (r, want) in enumerate(((0, first - 1), (ROWS - 1, first + ROWS))):
        for q in range(PAIRS):
            i, s = divmod(2 * q, NNZ)
            j, u = divmod(min(2 * q + 1, MAT * NNZ - 1), NNZ)
            a = (cols_ref[s, r, i] == want).astype(jnp.float32)
            b = (cols_ref[u, r, j] == want).astype(jnp.float32)
            mask_ref[side, :, pl.ds(q * LANES, LANES)] = jnp.where(few, a, b)


def outer(beside_ref, across_ref, end_hi, end_lo, mask_ref, part_ref, out_ref, lhs):
    even = lax.rem(lax.axis_index("node"), 2) == 0
    near = lefts(STEP)
    for side in range(2):
        even_ref, odd_ref = (across_ref, beside_ref.at[0]) if side == 0 else (beside_ref.at[1], across_ref)
        both = []
        for k in range(TWOS):
            packed = jnp.where(even, even_ref[k], odd_ref[k])
            turned = pltpu.roll(packed, BLOCK, 1)
            first, second = jnp.where(near, packed, turned), jnp.where(near, turned, packed)
            both += [first, second]
        for q in range(PAIRS):
            i, j = 2 * q // NNZ, min(2 * q + 1, MAT * NNZ - 1) // NNZ
            value = both[i] if i == j else jnp.where(near, both[i], both[j])
            mask = mask_ref[side, :, pl.ds(q * LANES, LANES)]
            value = jnp.where(jnp.concatenate([mask] * (STEP // 8), axis=0) != 0.0, value, 0.0)
            hi, lo = split(value)
            lhs[pl.ds(side * PAD, STEP), pl.ds(q * LANES, LANES)] = hi
            lhs[pl.ds((2 + side) * PAD, STEP), pl.ds(q * LANES, LANES)] = lo
    twos = jnp.dot(lhs[:, :DEPTH], end_hi[...], preferred_element_type=jnp.float32)
    total = twos[: 2 * PAD] + twos[2 * PAD :]
    total = total + jnp.dot(lhs[: 2 * PAD, :DEPTH], end_lo[...], preferred_element_type=jnp.float32)
    left = lefts(OWN)
    out_ref[...] = part_ref[...]
    out_ref[:, :LANES] = part_ref[:, :LANES] + jnp.where(left, total[:OWN], 0.0)
    out_ref[:, NODES - LANES :] = part_ref[:, NODES - LANES :] + jnp.where(left, 0.0, total[PAD : PAD + OWN])


def shards(panels, blocks, cols):
    count = lax.axis_size("node")
    gathered = lax.all_gather(panels, "mode", axis=0, tiled=False)
    cols = cols.transpose(1, 2, 0)
    vmem = pl.BlockSpec(memory_space=pltpu.VMEM)
    smem = pl.BlockSpec(memory_space=pltpu.SMEM)
    f32, bf16 = jnp.float32, jnp.bfloat16
    params = pltpu.CompilerParams(vmem_limit_bytes=24 << 20)
    mixed = jax.ShapeDtypeStruct((MAT, SLOTS, PAD, LANES), bf16)
    edge = jax.ShapeDtypeStruct((TWOS, STEP, LANES), f32)
    mixed_hi, mixed_lo, across, beside = pl.pallas_call(
        mix,
        out_shape=(mixed, mixed, edge, edge),
        in_specs=[vmem],
        out_specs=(vmem,) * 4,
        scratch_shapes=[
            pltpu.VMEM((GROUPS * STEP, NODES), f32),
            pltpu.VMEM((VARS * STEP, GROUPS * STEP), f32),
            pltpu.VMEM((2, MAT, STEP, LANES), f32),
        ],
        compiler_params=params,
        cost_estimate=pl.CostEstimate(flops=4_000_000_000, bytes_accessed=20_000_000, transcendentals=0),
    )(gathered)
    steps = [(i, i + 1) for i in range(1, count - 1, 2)]
    across = lax.ppermute(across, "node", steps + [(b, a) for a, b in steps])
    beside = lax.all_gather(beside, "node", axis=0, axis_index_groups=[[i, i + 1] for i in range(0, count, 2)])
    end = jax.ShapeDtypeStruct((DEPTH, LANES), bf16)
    mask = jax.ShapeDtypeStruct((2, 8, PAIRS * LANES), f32)
    part, end_hi, end_lo, mask = pl.pallas_call(
        inner,
        out_shape=(jax.ShapeDtypeStruct(panels.shape, f32), end, end, mask),
        in_specs=[smem, vmem, vmem, vmem],
        out_specs=(vmem,) * 4,
        scratch_shapes=[
            pltpu.VMEM((2, 8 * PAD, PAIRS * LANES), bf16),
        ],
        compiler_params=params,
        cost_estimate=pl.CostEstimate(flops=900_000_000, bytes_accessed=8_000_000, transcendentals=0),
    )(cols, mixed_hi, mixed_lo, blocks.reshape(DEPTH, NODES))
    return pl.pallas_call(
        outer,
        out_shape=jax.ShapeDtypeStruct(panels.shape, f32),
        in_specs=[vmem] * 6,
        out_specs=vmem,
        scratch_shapes=[pltpu.VMEM((4 * PAD, PAIRS * LANES), bf16)],
        compiler_params=params,
        cost_estimate=pl.CostEstimate(flops=100_000_000, bytes_accessed=1_500_000, transcendentals=0),
    )(beside, across, end_hi, end_lo, mask, part)


def solution(mesh):
    return jax.shard_map(
        shards,
        mesh=mesh,
        in_specs=(P("mode", "node"), P(None, None, None, "node"), P(None, None, "node")),
        out_specs=P("mode", "node"),
        check_vma=False,
    )
```

time: 54.4 us -> 51.7 us (0.950)
  blocking collectives: 34.2 us -> 36.2 us
  Pallas kernels: 6.45 us -> 4.49 us
  starting transfers between devices: 12.7 us -> 10.8 us
  local copies, waits for them, and re-layouts: 0.7 us -> 0.01 us
    ppermute x1 -> x0, starting transfers between devices: 1.92 us -> none  [shards(): beside = lax.ppermute(beside, 'node', [(i, i ^ 1) for i in range(count)])]
    all_gather x0 -> x1, blocking collectives: none -> 1.91 us  [shards(): lax.all_gather(beside, 'node', axis=0, axis_index_groups=[[i, i + 1] for...]
    pallas_call x1, Pallas kernels: 3.48 us -> 2.52 us  [shards(): pl.pallas_call(inner, out_shape=(jax.ShapeDtypeStruct(panels.shape, f32),...]
    pallas_call x1, Pallas kernels: 1.84 us -> 1.1 us  [shards(): pl.pallas_call(outer, out_shape=jax.ShapeDtypeStruct(panels.shape, f32),...]
    unnamed x2 -> x6, local copies, waits for them, and re-layouts: 0.7 us -> 0.01 us
  transfers between devices with their start and end apart: 2 -> 1, of which waited for: 0 -> 0; matrix products, arithmetic and copies ran while one was open for 0% -> 0% of each run, Pallas kernels for 6% -> 5%
where the time goes in v3:
time: 51.7 us; the launch traced here: 51.6 us
  blocking collectives  36.2 us (70%)
  starting transfers between devices  10.8 us (21%)
  Pallas kernels  4.49 us (9%)
    all_gather x1, blocking collectives, shards(): gathered = lax.all_gather(panels, 'mode', axis=0, tiled=False)  34.3 us
    ppermute x1, starting transfers between devices, shards(): across = lax.ppermute(across, 'node', steps + [(b, a) for a, b in steps])  10.8 us
    pallas_call x1, Pallas kernels, shards(): pl.pallas_call(inner, out_shape=(jax.ShapeDtypeStruct(panels.shape, f32),...  2.52 us
    all_gather x1, blocking collectives, shards(): lax.all_gather(beside, 'node', axis=0, axis_index_groups=[[i, i + 1] for...  1.91 us
    pallas_call x1, Pallas kernels, shards(): pl.pallas_call(outer, out_shape=jax.ShapeDtypeStruct(panels.shape, f32),...  1.1 us
  transfers between devices with their start and end apart: 1, of which 0 were waited for; matrix products, arithmetic and copies ran while one was open for 0% of the time, Pallas kernels for 5%

profile of v3, /device:TPU:1, one launch (start us, length us, event | category | flops | bytes accessed | tf_op | source)
XLA Modules:
  0.0 51.6 jit_solution(7525786741545338072)
XLA Ops:
  0.0 0.0 slice-start
  0.0 34.3 %all-gather.2.gathered_ref = f32[16,18,512]{2,1,0:T(8,128)S(1)} all-gather(f32[1,18,512]{2,1,0:T(8,128)} %bitcast.9), channel_id=2, replica_groups=mesh['node'=32,'mode'=16] {'mode'}, dimensions={0}, use_global_device_ids=true | all-gather | bytes 626688 | tf_op jit(solution)/shard_map/all_gather | solution.py:215
  34.3 0.0 slice-start.1
  34.3 0.0 copy-start
  34.3 0.9 %shard_map.37 = (bf16[11,10,32,128]{3,2,1,0:T(8,128)(2,1)S(1)}, bf16[11,10,32,128]{3,2,1,0:T(8,128)(2,1)S(1)}, f32[6,24,128]{2,1,0:T(8,128)S(1)}, f32[6,24,128]{2,1,0:T(8,128)S(1)}) custom-call(f32[16,18,512]{2,1,0:T(8,128)S(1)} %all-gather.2.gathered_ref), custom_call_target="tpu_custom_call" | custom-call | flops 4000000000 | bytes 20000000 | tf_op jit(solution)/shard_map/pallas_call | solution.py:223
  35.2 10.8 %collective-permute-start = (f32[6,24,128]{2,1,0:T(8,128)S(1)}, f32[6,24,128]{2,1,0:T(8,128)S(1)}, u32[]{:S(2)}, u32[]{:S(2)}) collective-permute-start(f32[6,24,128]{2,1,0:T(8,128)S(1)} %get-tuple-element.14), channel_id=1, source_target_pairs={{16,32},{48,64},{80,96},{112,128},{144,160},{176,192},{208,224},{2... | collective-permute-start | bytes 221192 | tf_op jit(solution)/shard_map/ppermute | solution.py:237
  46.0 1.9 %all-gather.1 = f32[12,24,128]{2,1,0:T(8,128)S(1)} all-gather(f32[6,24,128]{2,1,0:T(8,128)S(1)} %get-tuple-element.13), channel_id=3, replica_groups={{0,16},{32,48},{64,80},{96,112},{128,144},{160,176},{192,208},{224,240}..., dimensions={0}, use_global_device_ids=true | all-gather | bytes 221184 | tf_op jit(solution)/shard_map/all_gather | solution.py:238
  47.9 0.0 slice-done
  47.9 0.0 slice-done.1
  47.9 0.0 copy-done
  48.0 2.5 %shard_map.38 = (f32[18,512]{1,0:T(8,128)S(1)}, bf16[2112,128]{1,0:T(8,128)(2,1)S(1)}, bf16[2112,128]{1,0:T(8,128)(2,1)S(1)}, f32[2,8,2176]{2,1,0:T(8,128)S(1)}) custom-call(s32[3,8,11]{2,1,0:T(8,128)S(1)} %bitcast.8, bf16[11,10,32,128]{3,2,1,0:T(8,128)(2,1)S(1)} %get-tuple-element.15.mixed_hi, bf16[11,10,32,128]{3,2,1,0:T(8,128)(2,1)S(1)} %get-tuple-element.16.mixed_lo, ...), custom_call_target="tpu_custom_call" | custom-call | flops 900000000 | bytes 8000000 | tf_op jit(solution)/shard_map/pallas_call | solution.py:241
  50.5 0.0 collective-permute-done.across_ref
  50.5 1.1 %shard_map.39 = f32[18,512]{1,0:T(8,128)} custom-call(f32[2,6,24,128]{3,2,1,0:T(8,128)S(1)} %bitcast.7, f32[6,24,128]{2,1,0:T(8,128)S(1)} %collective-permute-done.across_ref, bf16[2112,128]{1,0:T(8,128)(2,1)S(1)} %get-tuple-element.17.end_hi, bf16[2112,128]{1,0:T(8,128)(2,1)S(1)} %get-tuple-element.18.end_lo, f32[2,8,2176]{2,1,0:T(8,128)S(1)} %get-tuple-element.19.mask_ref, ...), custom_call_target="tpu_custom_call" | custom-call | flops 100000000 | bytes 1500000 | tf_op jit(solution)/shard_map/pallas_call | solution.py:252
  (1 shorter events, 0.0 us)
Async XLA Ops:
  0.0 47.9 %slice-start = ((s8[4325376]{0:T(1024)(128)(4,1)}), s8[4194304]{0:T(1024)(128)(4,1)S(1)}, s32[]{:S(2)}) async-start(s8[4325376]{0:T(1024)(128)(4,1)} %bitcast.4), calls=%async_computation | async-start | bytes 8388608
  34.3 13.6 %slice-start.1 = ((s8[4325376]{0:T(1024)(128)(4,1)}), s8[131072]{0:T(1024)(128)(4,1)S(1)}, s32[]{:S(2)}) async-start(s8[4325376]{0:T(1024)(128)(4,1)} %bitcast.4), calls=%async_computation.1 | async-start | bytes 262144
  34.3 13.6 %copy-start = (s32[11,3,8]{0,2,1:T(8,128)S(1)}, s32[11,3,8]{0,2,1:T(8,128)}, u32[]{:S(2)}) copy-start(s32[11,3,8]{0,2,1:T(8,128)} %param.5) | copy-start | bytes 3172
  35.2 15.3 %collective-permute-start = (f32[6,24,128]{2,1,0:T(8,128)S(1)}, f32[6,24,128]{2,1,0:T(8,128)S(1)}, u32[]{:S(2)}, u32[]{:S(2)}) collective-permute-start(f32[6,24,128]{2,1,0:T(8,128)S(1)} %get-tuple-element.14), channel_id=1, source_target_pairs={{16,32},{48,64},{80,96},{112,128},{144,160},{176,192},{208,224},{2... | collective-permute-start | bytes 221192 | tf_op jit(solution)/shard_map/ppermute | solution.py:237
